TPU v7x, 512 devices: a whole 4x4x16 slice. The times are simulated.
512 devices in a mesh: mem: 128 (over x, z, core), rep: 4 (over y).
Axes of the slice: x: 4, y: 4, z: 16, core: 2. Of those that a mesh axis runs over, the one named last changes fastest.
Arguments:
- states: bfloat16 [2048, 384], P('rep'), may hold values from -6 to 6
- batch_index: int32 [2, 2048], P(None, 'rep'), may hold values from 0 to 511
- obs_pick: int32 [2, 128], replicated, may hold values from 0 to 383
- norm_gain: float32 [384], replicated, may hold values from 0.5 to 1.5
- w_in: bfloat16 [384, 1024], replicated, may hold values from -0.3125 to 0.3125
- b_in: float32 [1024], replicated, may hold values from -0.5 to 0.5
- member_params: bfloat16 [128, 393216], P('mem', 'rep'), may hold values from -6 to 6
- observed: bfloat16 [2, 2048, 128], P(None, 'rep'), may hold values from -6 to 6
- perturbation: bfloat16 [128, 2, 2048, 128], P('mem', None, 'rep'), may hold values from -6 to 6
- inv_sigma: float32 [2, 2048, 128], P(None, 'rep'), may hold values from 0.5 to 4
Outputs:
- updated_params: bfloat16 [128, 393216], P('mem', 'rep')
Inputs may be any that keep to these rules, and one draw needn't show every extreme that they name: `batch_index`: row number of a start state inside the block of 512 given states that belongs to its block of 512 batch rows. `obs_pick`: observed feature numbers; a number may repeat.
All inputs are finite; a program needn't handle non-finite values.
Results may differ from a plain program's by a relative error of at most 0.0056.
Values may be sent and summed in bfloat16 or wider, within the bound.
No kernel may reach another device: no remote copies, remote signals or barrier semaphores. Data moves between devices by JAX's collectives and lax.ppermute only.
A program may use at most 64 MiB of HBM per device.

v0:
```python
import jax
import jax.numpy as jnp
from jax import lax
from jax.sharding import PartitionSpec as P

EPS = 1e-06
DT = 0.5


def hidden_layer(state, norm_gain, w_in, b_in):
    normed = (
        state * lax.rsqrt(jnp.mean(state * state, axis=-1, keepdims=True) + EPS) * norm_gain
    ).astype(jnp.bfloat16)
    return jax.nn.gelu(jnp.dot(normed, w_in, preferred_element_type=jnp.float32) + b_in).astype(
        jnp.bfloat16
    )


def member_sums(pieces):
    weighted, misfit_w = pieces
    count = weighted.shape[0]
    gram_list = []
    innov_list = []
    for item_index in range(weighted.shape[1]):
        flat = weighted[:, item_index].reshape(count, -1).astype(jnp.float32)
        anomaly = (flat - jnp.mean(flat, axis=0)).astype(jnp.bfloat16)
        misfit_flat = misfit_w[:, item_index].reshape(count, -1)
        gram_list.append(
            lax.dot_general(
                anomaly, anomaly, (((1,), (1,)), ((), ())), preferred_element_type=jnp.float32
            )
        )
        innov_list.append(
            lax.dot_general(
                anomaly, misfit_flat, (((1,), (1,)), ((), ())), preferred_element_type=jnp.float32
            )
        )
    return (jnp.stack(gram_list, axis=0), jnp.stack(innov_list, axis=0))


def solve_columns(system, right_side):
    lower_factor = jnp.linalg.cholesky(system)
    halfway = lax.linalg.triangular_solve(lower_factor, right_side, left_side=True, lower=True)
    return lax.linalg.triangular_solve(
        lower_factor, halfway, left_side=True, lower=True, transpose_a=True
    )


def on_device(
    states,
    batch_index,
    obs_pick,
    norm_gain,
    w_in,
    b_in,
    member_params,
    observed,
    perturbation,
    inv_sigma,
):
    local_members = member_params.shape[0]
    width = w_in.shape[1]
    features = w_in.shape[0]
    step_count = batch_index.shape[0]
    picked = obs_pick.shape[1]
    whole_params = lax.all_gather(member_params, "rep", axis=1, tiled=True)
    weights = whole_params.reshape(local_members, width, features)
    step_scale = DT * width ** (-0.5)
    start_state = jnp.take(states, batch_index, axis=0).astype(jnp.float32)
    shared = hidden_layer(start_state, norm_gain, w_in, b_in)
    current = start_state[None] + step_scale * jnp.einsum(
        "kbh,jhs->jkbs", shared, weights, preferred_element_type=jnp.float32
    )
    layer = hidden_layer(current, norm_gain, w_in, b_in)
    current = current + step_scale * jnp.einsum(
        "jkbh,jhs->jkbs", layer, weights, preferred_element_type=jnp.float32
    )
    feature_ids = lax.broadcasted_iota(jnp.int32, (step_count, features, picked), 1)
    selector = (feature_ids == obs_pick[:, None, :]).astype(jnp.float32)
    predicted = jnp.einsum("jkbs,ksf->jkbf", current, selector, precision=lax.Precision.HIGHEST)
    weighted = (predicted * inv_sigma).astype(jnp.bfloat16)
    misfit_w = (
        observed.astype(jnp.float32) * inv_sigma
        + perturbation.astype(jnp.float32)
        - predicted * inv_sigma
    ).astype(jnp.bfloat16)
    misfit_local = jnp.sum(jnp.square(misfit_w.astype(jnp.float32)))
    gram_items, innov_items = member_sums(
        (
            lax.all_to_all(weighted, "mem", split_axis=2, concat_axis=0, tiled=True),
            lax.all_to_all(misfit_w, "mem", split_axis=2, concat_axis=0, tiled=True),
        )
    )
    gram_matrix = jnp.sum(gram_items, axis=0)
    innovation = jnp.sum(innov_items, axis=0)
    members = gram_matrix.shape[0]
    entries = members * step_count * batch_index.shape[1] * lax.axis_size("rep") * picked
    identity = jnp.eye(members, dtype=jnp.float32)
    gram_matrix, innovation, misfit_total = lax.psum(
        (gram_matrix, innovation, misfit_local), ("mem", "rep")
    )
    system = gram_matrix + (1.0 + misfit_total / entries) * (members - 1) * identity
    coefficients = solve_columns(system, innovation)
    param_block = lax.all_to_all(member_params, "mem", split_axis=1, concat_axis=0, tiled=True)
    params_f = param_block.astype(jnp.float32)
    spread = params_f - jnp.mean(params_f, axis=0)
    change = jnp.einsum("kj,kp->jp", coefficients, spread, precision=lax.Precision.HIGHEST)
    renewed = (params_f + change).astype(jnp.bfloat16)
    return lax.all_to_all(renewed, "mem", split_axis=0, concat_axis=1, tiled=True)


def solution(mesh):
    placed = (
        P("rep", None),
        P(None, "rep"),
        P(),
        P(),
        P(),
        P(),
        P("mem", "rep"),
        P(None, "rep", None),
        P("mem", None, "rep", None),
        P(None, "rep", None),
    )
    return jax.shard_map(
        on_device, mesh=mesh, in_specs=placed, out_specs=P("mem", "rep"), check_vma=False
    )
```

profile of v0, /device:TPU:8, one launch (start us, length us, event | category | flops | bytes accessed | tf_op | source)
XLA Modules:
  0.0 755.3 jit_solution(18304707724078509563)
XLA Ops:
  6.5 0.6 broadcast.183
  7.1 2.8 reduce.16
  9.9 0.7 reshape.213
  10.6 20.2 %all-to-all-start = ((bf16[128,2,384]{2,1,0:T(2,128)(2,1)}), bf16[128,2,384]{2,1,0:T(2,128)(2,1)}, u32[]{:S(2)}, u32[]{:S(2)}) async-start(bf16[128,2,384]{2,1,0:T(2,128)(2,1)} %reshape.213), calls=%async_computation | async-start | bytes 393216 | tf_op jit(solution)/shard_map/all_to_all | solution.py:104
  30.9 0.7 fusion.75
  31.5 0.7 compare_and_fusion
  32.2 17.5 %all_gather.3 = bf16[1,393216]{1,0:T(2,128)(2,1)S(1)} all-gather(bf16[1,98304]{1,0:T(2,128)(2,1)S(1)} %copy-done.2), channel_id=1, replica_groups=mesh['mem'=128,'rep'=4] {'rep'}, dimensions={1}, use_global_device_ids=true | all-gather | bytes 983040 | tf_op jit(solution)/shard_map/all_gather | solution.py:66
  49.8 16.3 %reduce.14 = bf16[393216]{0:T(1024)(128)(2,1)S(1)} reduce(bf16[1,393216]{1,0:T(2,128)(2,1)S(1)} %all_gather.3, bf16[]{:T(256)} %constant.98), dimensions={0}, to_apply=%all_gather.3.reduce_sub_computation | reduce | bytes 1572866 | tf_op jit(solution)/shard_map/all_gather | solution.py:66
  66.1 1.2 reshape.185
  67.4 1.3 reshape.205
  68.6 4.1 gather_fusion
  72.8 0.4 fusion.16
  73.2 1.2 copy.38
  74.4 4.1 multiply_reduce_fusion
  78.6 1.2 copy.43
  79.9 0.1 copy.50
  80.0 1.8 copy.52
  81.8 5.2 fusion.25
  87.0 3.7 multiply_reduce_fusion.1
  90.7 1.8 copy.44
  92.5 16.3 %all-to-all-start.1 = ((bf16[1,2,512,128]{3,1,0,2:T(2,128)(2,1)}), bf16[1,2,512,128]{3,1,0,2:T(2,128)(2,1)S(1)}, u32[]{:S(2)}, u32[]{:S(2)}) async-start(bf16[1,2,512,128]{3,1,0,2:T(2,128)(2,1)} %copy.44), calls=%async_computation.1 | async-start | bytes 524288 | tf_op jit(solution)/shard_map/all_to_all | solution.py:90
  108.8 0.9 copy.54
  109.7 22.9 %all-to-all-done.1 = bf16[1,2,512,128]{3,1,0,2:T(2,128)(2,1)S(1)} async-done(((bf16[1,2,512,128]{3,1,0,2:T(2,128)(2,1)}), bf16[1,2,512,128]{3,1,0,2:T(2,128)(2,1)S(1)}, u32[]{:S(2)}, u32[]{:S(2)}) %all-to-all-start.1) | async-done | bytes 262176 | tf_op jit(solution)/shard_map/all_to_all | solution.py:90
  132.6 6.2 all-to-all-start.2
  138.7 0.0 all-reduce.3.cloned.1.call-start
  138.8 105.2 %psum.22 = f32[]{:T(128)} all-reduce(f32[]{:T(128)} %get-tuple-element.9), channel_id=1, replica_groups=mesh['mem'=128,'rep'=4] {'mem','rep'}, use_global_device_ids=true, to_apply=%region_6.7 | all-reduce | flops 1 | bytes 8 | tf_op jit(solution)/shard_map/psum | solution.py:99
  244.6 1.6 reshape.214
  246.3 0.1 convert_reduce_fusion.2
  246.5 0.1 fusion.63
  246.6 0.2 convolution_bitcast_fusion.2
  246.8 0.2 convolution_bitcast_fusion
  247.0 0.8 fusion.31
  247.8 0.8 fusion.32
  248.7 442.5 %all-reduce.3.cloned.1.call-done = (f32[128,128]{1,0:T(8,128)}, f32[128,128]{1,0:T(8,128)}) async-done(((f32[128,128]{1,0:T(8,128)}, f32[128,128]{1,0:T(8,128)}), (f32[128,128]{1,0:T(8,128)}, f32[128,128]{1,0:T(8,128)})) %all-reduce.3.cloned.1.call-update) | async-done | bytes 131088 | tf_op jit(solution)/shard_map/psum | solution.py:99
  691.2 0.9 select_add_fusion
  692.1 0.1 copy.53
  692.2 0.9 fusion.74
  693.0 11.7 %cholesky.16 = f32[128,128]{1,0:T(8,128)S(1)} custom-call(f32[128,128]{1,0:T(8,128)S(1)} %fusion.74), custom_call_target="Cholesky" | custom-call | tf_op jit(solution)/shard_map/jit(cholesky)/cholesky | solution.py:42
  704.8 0.6 compare_reduce_fusion
  705.4 0.7 fusion.69
  706.1 9.8 %custom-call.8 = f32[1,128,128]{1,2,0:T(8,128)S(1)} custom-call(f32[1,128,128]{2,1,0:T(8,128)S(1)} %fusion.69), custom_call_target="InvertDiagBlocksLowerTriangular" | custom-call | tf_op jit(solution)/shard_map/triangular_solve | solution.py:44
  715.9 1.1 fusion.72
  717.0 0.2 fusion.70
  717.2 0.5 fusion.30
  717.8 0.8 reduce.17
  718.5 0.1 reshape.215
  718.6 28.9 %all_to_all.65 = bf16[128,2,384]{2,1,0:T(2,128)(2,1)S(1)} all-to-all(bf16[128,2,384]{2,1,0:T(2,128)(2,1)S(1)} %reshape.215), channel_id=1, replica_groups=mesh['mem'=128,'rep'=4] {'mem'}, dimensions={0} | all-to-all | bytes 393216 | tf_op jit(solution)/shard_map/all_to_all | solution.py:109
  747.5 0.9 reshape.216
  (27 shorter events, 0.2 us)
Async XLA Ops:
  6.5 67.9 %copy-start = (bf16[384,1024]{1,0:T(8,128)(2,1)S(1)}, bf16[384,1024]{1,0:T(8,128)(2,1)}, u32[]{:S(2)}) copy-start(bf16[384,1024]{1,0:T(8,128)(2,1)} %param.14) | copy-start | bytes 2359300
  6.5 25.7 %copy-start.2 = (bf16[1,98304]{1,0:T(2,128)(2,1)S(1)}, bf16[1,98304]{1,0:T(2,128)(2,1)}, u32[]{:S(2)}) copy-start(bf16[1,98304]{1,0:T(2,128)(2,1)} %param.16) | copy-start | bytes 589828
  10.6 81.9 %all-to-all-start = ((bf16[128,2,384]{2,1,0:T(2,128)(2,1)}), bf16[128,2,384]{2,1,0:T(2,128)(2,1)}, u32[]{:S(2)}, u32[]{:S(2)}) async-start(bf16[128,2,384]{2,1,0:T(2,128)(2,1)} %reshape.213), calls=%async_computation | async-start | bytes 393216 | tf_op jit(solution)/shard_map/all_to_all | solution.py:104
  66.1 2.5 copy-start.1
  72.7 1.7 copy-start.5
  72.7 1.7 copy-start.6
  74.4 5.4 copy-start.3
  81.8 5.2 copy-start.4
  92.5 40.0 %all-to-all-start.1 = ((bf16[1,2,512,128]{3,1,0,2:T(2,128)(2,1)}), bf16[1,2,512,128]{3,1,0,2:T(2,128)(2,1)S(1)}, u32[]{:S(2)}, u32[]{:S(2)}) async-start(bf16[1,2,512,128]{3,1,0,2:T(2,128)(2,1)} %copy.44), calls=%async_computation.1 | async-start | bytes 524288 | tf_op jit(solution)/shard_map/all_to_all | solution.py:90
  132.6 114.2 %all-to-all-start.2 = ((bf16[1,2,512,128]{3,1,0,2:T(2,128)(2,1)}), bf16[1,2,512,128]{3,1,0,2:T(2,128)(2,1)S(1)}, u32[]{:S(2)}, u32[]{:S(2)}) async-start(bf16[1,2,512,128]{3,1,0,2:T(2,128)(2,1)} %copy.54), calls=%async_computation.2 | async-start | bytes 524288 | tf_op jit(solution)/shard_map/all_to_all | solution.py:91
  138.7 552.5 %all-reduce.3.cloned.1.call-start = ((), (), s32[]{:S(2)}) async-start(), calls=%async_computation.4 | async-start | bytes 262144 | tf_op jit(solution)/shard_map/psum | solution.py:99
Sparse Core Ops, SparseCore 0:
  248.8 442.3 all-reduce.2
where the time goes:
time: 756 us; the launch traced here: 755 us
  waiting for transfers between devices  465 us (62%)
  blocking collectives  152 us (20%)
  other arithmetic  46.5 us (6%)
  starting transfers between devices  42.8 us (6%)
  local copies, waits for them, and re-layouts  17.6 us (2%)
  matrix products  16.9 us (2%)
  between operations  14.3 us (2%)
    psum x1, waiting for transfers between devices, on_device(): lax.psum((gram_matrix, innovation, misfit_local), ('mem', 'rep'))  443 us
    psum x1, blocking collectives, on_device(): lax.psum((gram_matrix, innovation, misfit_local), ('mem', 'rep'))  105 us
    all_to_all x1, blocking collectives, on_device(): lax.all_to_all(renewed, 'mem', split_axis=0, concat_axis=1, tiled=True)  28.9 us
    all_to_all x1, waiting for transfers between devices, on_device(): lax.all_to_all(weighted, 'mem', split_axis=2, concat_axis=0, tiled=True)  22.9 us
    all_to_all x1, starting transfers between devices, on_device(): lax.all_to_all(member_params, 'mem', split_axis=1, concat_axis=0, tiled=T...  20.2 us
    all_gather x1, blocking collectives, on_device(): whole_params = lax.all_gather(member_params, 'rep', axis=1, tiled=True)  17.5 us
    all_gather x1, other arithmetic, on_device(): whole_params = lax.all_gather(member_params, 'rep', axis=1, tiled=True)  16.3 us
    all_to_all x1, starting transfers between devices, on_device(): lax.all_to_all(weighted, 'mem', split_axis=2, concat_axis=0, tiled=True)  16.3 us
  transfers between devices with their start and end apart: 4, of which 2 were waited for; matrix products, arithmetic and copies ran while one was open for 6% of the time, Pallas kernels for 0%

commit v1 on v0

--- a/solution.py
+++ b/solution.py
@@ -1,3 +1,4 @@
+import functools
 import jax
 import jax.numpy as jnp
 from jax import lax
@@ -5,6 +6,15 @@
 
 EPS = 1e-06
 DT = 0.5
+
+
+def _draw_levels_all(row_data, lane_axis, net_axis):
+    for j0 in (lane_axis, net_axis):
+        row_data = jax.lax.psum(row_data, j0)
+    return row_data
+
+
+extend_stocks = functools.partial(_draw_levels_all, lane_axis="mem", net_axis="rep")
 
 
 def hidden_layer(state, norm_gain, w_in, b_in):
@@ -96,9 +106,7 @@
     members = gram_matrix.shape[0]
     entries = members * step_count * batch_index.shape[1] * lax.axis_size("rep") * picked
     identity = jnp.eye(members, dtype=jnp.float32)
-    gram_matrix, innovation, misfit_total = lax.psum(
-        (gram_matrix, innovation, misfit_local), ("mem", "rep")
-    )
+    gram_matrix, innovation, misfit_total = extend_stocks((gram_matrix, innovation, misfit_local))
     system = gram_matrix + (1.0 + misfit_total / entries) * (members - 1) * identity
     coefficients = solve_columns(system, innovation)
     param_block = lax.all_to_all(member_params, "mem", split_axis=1, concat_axis=0, tiled=True)

time: 756 us -> 838 us (1.11)
  the two profiles are of different devices: /device:TPU:8 before, /device:TPU:1 now
where the time goes in v1:
time: 838 us; the launch traced here: 837 us
  waiting for transfers between devices  379 us (45%)
  blocking collectives  316 us (38%)
  starting transfers between devices  46.7 us (6%)
  other arithmetic  46.5 us (6%)
  local copies, waits for them, and re-layouts  17.7 us (2%)
  matrix products  16.9 us (2%)
  between operations  14.3 us (2%)
    psum x2, waiting for transfers between devices, _draw_levels_all(): row_data = jax.lax.psum(row_data, j0)  357 us
    psum x2, blocking collectives, _draw_levels_all(): row_data = jax.lax.psum(row_data, j0)  261 us
    all_to_all x1, blocking collectives, on_device(): lax.all_to_all(renewed, 'mem', split_axis=0, concat_axis=1, tiled=True)  38.4 us
    all_to_all x1, waiting for transfers between devices, on_device(): lax.all_to_all(weighted, 'mem', split_axis=2, concat_axis=0, tiled=True)  21.6 us
    all_to_all x1, starting transfers between devices, on_device(): lax.all_to_all(member_params, 'mem', split_axis=1, concat_axis=0, tiled=T...  20.8 us
    all_to_all x1, starting transfers between devices, on_device(): lax.all_to_all(weighted, 'mem', split_axis=2, concat_axis=0, tiled=True)  18.6 us
  transfers between devices with their start and end apart: 5, of which 3 were waited for; matrix products, arithmetic and copies ran while one was open for 6% of the time, Pallas kernels for 0%

profile of v1, /device:TPU:1, one launch (start us, length us, event | category | flops | bytes accessed | tf_op | source)
XLA Modules:
  0.0 837.3 jit_solution(652323702125672614)
XLA Ops:
  6.5 0.6 broadcast.183
  7.1 2.8 reduce.16
  9.9 0.7 reshape.213
  10.6 20.8 %all-to-all-start = ((bf16[128,2,384]{2,1,0:T(2,128)(2,1)}), bf16[128,2,384]{2,1,0:T(2,128)(2,1)}, u32[]{:S(2)}, u32[]{:S(2)}) async-start(bf16[128,2,384]{2,1,0:T(2,128)(2,1)} %reshape.213), calls=%async_computation | async-start | bytes 393216 | tf_op jit(solution)/shard_map/all_to_all | solution.py:112
  31.4 0.7 fusion.75
  32.1 0.7 compare_and_fusion
  32.8 16.5 %all_gather.3 = bf16[1,393216]{1,0:T(2,128)(2,1)S(1)} all-gather(bf16[1,98304]{1,0:T(2,128)(2,1)S(1)} %copy-done.2), channel_id=1, replica_groups=mesh['mem'=128,'rep'=4] {'rep'}, dimensions={1}, use_global_device_ids=true | all-gather | bytes 983040 | tf_op jit(solution)/shard_map/all_gather | solution.py:76
  49.3 16.3 %reduce.14 = bf16[393216]{0:T(1024)(128)(2,1)S(1)} reduce(bf16[1,393216]{1,0:T(2,128)(2,1)S(1)} %all_gather.3, bf16[]{:T(256)} %constant.98), dimensions={0}, to_apply=%all_gather.3.reduce_sub_computation | reduce | bytes 1572866 | tf_op jit(solution)/shard_map/all_gather | solution.py:76
  65.6 1.2 reshape.185
  66.9 1.3 reshape.205
  68.1 4.1 gather_fusion
  72.2 0.4 fusion.16
  72.7 1.2 copy.38
  73.9 4.1 multiply_reduce_fusion
  78.1 1.3 copy.43
  79.3 1.1 copy.50
  80.5 0.9 copy.52
  81.3 5.2 fusion.25
  86.5 3.7 multiply_reduce_fusion.1
  90.2 1.8 copy.44
  92.0 18.6 %all-to-all-start.1 = ((bf16[1,2,512,128]{3,1,0,2:T(2,128)(2,1)}), bf16[1,2,512,128]{3,1,0,2:T(2,128)(2,1)S(1)}, u32[]{:S(2)}, u32[]{:S(2)}) async-start(bf16[1,2,512,128]{3,1,0,2:T(2,128)(2,1)} %copy.44), calls=%async_computation.1 | async-start | bytes 524288 | tf_op jit(solution)/shard_map/all_to_all | solution.py:100
  110.6 0.9 copy.54
  111.5 21.6 %all-to-all-done.1 = bf16[1,2,512,128]{3,1,0,2:T(2,128)(2,1)S(1)} async-done(((bf16[1,2,512,128]{3,1,0,2:T(2,128)(2,1)}), bf16[1,2,512,128]{3,1,0,2:T(2,128)(2,1)S(1)}, u32[]{:S(2)}, u32[]{:S(2)}) %all-to-all-start.1) | async-done | bytes 262176 | tf_op jit(solution)/shard_map/all_to_all | solution.py:100
  133.1 7.3 all-to-all-start.2
  140.5 253.2 %psum.44 = f32[]{:T(128)} all-reduce(f32[]{:T(128)} %get-tuple-element.11), channel_id=1, replica_groups=mesh['mem'=128,'rep'=4] {'mem'}, use_global_device_ids=true, to_apply=%region_7.8 | all-reduce | flops 1 | bytes 8 | tf_op jit(solution)/shard_map/psum | solution.py:13
  393.7 8.0 psum.45
  402.3 1.6 reshape.214
  403.9 0.1 convert_reduce_fusion.2
  404.0 0.1 fusion.63
  404.2 0.2 convolution_bitcast_fusion.2
  404.4 0.2 convolution_bitcast_fusion
  404.6 0.8 fusion.31
  405.4 0.8 fusion.32
  406.4 307.6 %all-reduce.5.cloned.1.call-done = (f32[128,128]{1,0:T(8,128)}, f32[128,128]{1,0:T(8,128)}) async-done(((f32[128,128]{1,0:T(8,128)}, f32[128,128]{1,0:T(8,128)}), (f32[128,128]{1,0:T(8,128)}, f32[128,128]{1,0:T(8,128)})) %all-reduce.5.cloned.1.call-update) | async-done | bytes 131088 | tf_op jit(solution)/shard_map/psum | solution.py:13
  714.0 49.9 %all-reduce.7.cloned.1.call-done = (f32[128,128]{1,0:T(8,128)}, f32[128,128]{1,0:T(8,128)}) async-done(((f32[128,128]{1,0:T(8,128)}, f32[128,128]{1,0:T(8,128)}), (f32[128,128]{1,0:T(8,128)}, f32[128,128]{1,0:T(8,128)})) %all-reduce.7.cloned.1.call-update) | async-done | bytes 131088 | tf_op jit(solution)/shard_map/psum | solution.py:13
  763.9 0.9 select_add_fusion
  764.7 0.1 copy.53
  764.8 0.9 fusion.74
  765.7 11.7 %cholesky.16 = f32[128,128]{1,0:T(8,128)S(1)} custom-call(f32[128,128]{1,0:T(8,128)S(1)} %fusion.74), custom_call_target="Cholesky" | custom-call | tf_op jit(solution)/shard_map/jit(cholesky)/cholesky | solution.py:52
  777.4 0.6 compare_reduce_fusion
  778.1 0.7 fusion.69
  778.7 9.8 %custom-call.8 = f32[1,128,128]{1,2,0:T(8,128)S(1)} custom-call(f32[1,128,128]{2,1,0:T(8,128)S(1)} %fusion.69), custom_call_target="InvertDiagBlocksLowerTriangular" | custom-call | tf_op jit(solution)/shard_map/triangular_solve | solution.py:54
  788.5 1.1 fusion.72
  789.7 0.2 fusion.70
  789.9 0.5 fusion.30
  790.4 0.8 reduce.17
  791.2 38.4 %all_to_all.65 = bf16[128,2,384]{2,1,0:T(2,128)(2,1)S(1)} all-to-all(bf16[128,2,384]{2,1,0:T(2,128)(2,1)S(1)} %reshape.215), channel_id=1, replica_groups=mesh['mem'=128,'rep'=4] {'mem'}, dimensions={0} | all-to-all | bytes 393216 | tf_op jit(solution)/shard_map/all_to_all | solution.py:117
  829.6 0.9 reshape.216
  (31 shorter events, 0.4 us)
Async XLA Ops:
  6.5 67.4 %copy-start = (bf16[384,1024]{1,0:T(8,128)(2,1)S(1)}, bf16[384,1024]{1,0:T(8,128)(2,1)}, u32[]{:S(2)}) copy-start(bf16[384,1024]{1,0:T(8,128)(2,1)} %param.14) | copy-start | bytes 2359300
  6.5 26.3 %copy-start.2 = (bf16[1,98304]{1,0:T(2,128)(2,1)S(1)}, bf16[1,98304]{1,0:T(2,128)(2,1)}, u32[]{:S(2)}) copy-start(bf16[1,98304]{1,0:T(2,128)(2,1)} %param.16) | copy-start | bytes 589828
  10.6 81.4 %all-to-all-start = ((bf16[128,2,384]{2,1,0:T(2,128)(2,1)}), bf16[128,2,384]{2,1,0:T(2,128)(2,1)}, u32[]{:S(2)}, u32[]{:S(2)}) async-start(bf16[128,2,384]{2,1,0:T(2,128)(2,1)} %reshape.213), calls=%async_computation | async-start | bytes 393216 | tf_op jit(solution)/shard_map/all_to_all | solution.py:112
  65.6 2.5 copy-start.1
  72.2 1.7 copy-start.5
  72.2 1.7 copy-start.6
  78.0 2.4 copy-start.3
  81.3 5.2 copy-start.4
  92.0 41.1 %all-to-all-start.1 = ((bf16[1,2,512,128]{3,1,0,2:T(2,128)(2,1)}), bf16[1,2,512,128]{3,1,0,2:T(2,128)(2,1)S(1)}, u32[]{:S(2)}, u32[]{:S(2)}) async-start(bf16[1,2,512,128]{3,1,0,2:T(2,128)(2,1)} %copy.44), calls=%async_computation.1 | async-start | bytes 524288 | tf_op jit(solution)/shard_map/all_to_all | solution.py:100
  133.1 271.2 %all-to-all-start.2 = ((bf16[1,2,512,128]{3,1,0,2:T(2,128)(2,1)}), bf16[1,2,512,128]{3,1,0,2:T(2,128)(2,1)S(1)}, u32[]{:S(2)}, u32[]{:S(2)}) async-start(bf16[1,2,512,128]{3,1,0,2:T(2,128)(2,1)} %copy.54), calls=%async_computation.2 | async-start | bytes 524288 | tf_op jit(solution)/shard_map/all_to_all | solution.py:101
  140.4 573.6 %all-reduce.5.cloned.1.call-start = ((), (), s32[]{:S(2)}) async-start(), calls=%async_computation.4 | async-start | bytes 262144 | tf_op jit(solution)/shard_map/psum | solution.py:13
  406.3 357.6 %all-reduce.7.cloned.1.call-start = ((), (), s32[]{:S(2)}) async-start(), calls=%async_computation.5 | async-start | bytes 262144 | tf_op jit(solution)/shard_map/psum | solution.py:13
Sparse Core Ops, SparseCore 0:
  406.4 307.5 all-reduce.4
  716.4 47.4 all-reduce.6
